TPU v7x, 512 devices: a whole 4x4x16 slice. The times are simulated.
512 devices in a mesh: row: 32 (over x_lo, z), col: 16 (over x_hi, y, core).
Axes of the slice: x: 4 (x_hi: 2, x_lo: 2; x = x_hi * 2 + x_lo), y: 4, z: 16, core: 2. Of those that a mesh axis runs over, the one named last changes fastest.
Arguments:
- elemental: bfloat16 [2, 512, 512, 512], P(None, 'row', 'col'), may hold values from -6 to 6
- perambulators: bfloat16 [512, 2, 512, 512], P(('row', 'col')), may hold values from -0.1875 to 0.1875
- source_owner: int32 [1], replicated, may hold values from 0 to 511
Outputs:
- contracted: float32 [2, 512, 512, 512], P(None, None, 'row', 'col')
All inputs are finite; a program needn't handle non-finite values.
Results may differ from a plain program's by a relative error of at most 0.0041.
Values may be sent and summed in bfloat16 or wider, within the bound.
A program may use at most 64 MiB of HBM per device.

v0:
```python
import jax
import jax.numpy as jnp
from jax import lax
from jax.sharding import PartitionSpec as P


def broadcast(block, axis, owner):
    block = jnp.where(lax.axis_index(axis) == owner, block, jnp.zeros_like(block))
    return lax.psum(block, axis)


def build_mixing(peramb):
    real_part = peramb[0]
    imag_part = peramb[1]
    width = real_part.shape[0]
    upper = jnp.concatenate([real_part, -imag_part], axis=1)
    lower = jnp.concatenate([imag_part, real_part], axis=1)
    full = jnp.concatenate([upper, lower], axis=0)
    return full.reshape(2, width, 2, width)


def per_device(elemental, perambulators, source_owner):
    owner = source_owner[0]
    mine = perambulators[0]
    chosen = broadcast(mine, ("row", "col"), owner)
    mixing = build_mixing(chosen)
    first = jnp.einsum("scrk,rijk->sijc", mixing, elemental, preferred_element_type=jnp.float32)
    first = first.astype(jnp.bfloat16)
    result = jnp.einsum(
        "sbrj,rijc->sbic",
        mixing,
        lax.all_to_all(first, "col", split_axis=3, concat_axis=2, tiled=True),
        preferred_element_type=jnp.float32,
    )
    second = result.astype(jnp.bfloat16)
    return jnp.einsum(
        "sari,rbic->sabc",
        mixing,
        lax.all_to_all(second, "row", split_axis=1, concat_axis=2, tiled=True),
        preferred_element_type=jnp.float32,
    )


def solution(mesh):
    in_specs = (P(None, "row", "col", None), P(("row", "col"), None, None, None), P())
    out_specs = P(None, None, "row", "col")
    return jax.shard_map(
        per_device, mesh=mesh, in_specs=in_specs, out_specs=out_specs, check_vma=False
    )
```

profile of v0, /device:TPU:1, one launch (start us, length us, event | category | flops | bytes accessed | tf_op | source)
XLA Modules:
  0.0 645.3 jit_solution(15336203867315880260)
XLA Ops:
  6.5 0.0 all-reduce.2.cloned.1.call-start
  7.2 1.1 select_bitcast_fusion
  8.2 0.0 all-reduce.2.cloned.1.call-update
  8.3 483.9 %all-reduce.2.cloned.1.call-done = bf16[2,512,512]{2,1,0:T(8,128)(2,1)} async-done(((bf16[2,512,512]{2,1,0:T(8,128)(2,1)}), bf16[2,512,512]{2,1,0:T(8,128)(2,1)}) %all-reduce.2.cloned.1.call-update) | async-done | bytes 1048592 | tf_op jit(solution)/shard_map/psum | solution.py:9
  492.2 1.1 fusion.13
  493.3 1.3 slice_bitcast_fusion
  494.5 0.3 maximum_maximum_fusion
  494.9 0.0 copy-start.2
  494.9 2.8 reshape.6
  497.6 0.0 copy-done.2
  497.6 2.9 fusion.8
  500.5 6.5 copy.17
  507.0 6.7 %reshape.17 = bf16[16,2,16384]{2,1,0:T(2,128)(2,1)S(1)} reshape(bf16[512,2,16,32]{3,2,1,0:T(8,128)(2,1)} %bitcast.48) | data formatting | bytes 2097152
  513.6 23.2 %all_to_all.36 = bf16[16,2,16384]{2,1,0:T(2,128)(2,1)S(1)} all-to-all(bf16[16,2,16384]{2,1,0:T(2,128)(2,1)S(1)} %reshape.17), channel_id=1, replica_groups=mesh['row'=32,'col'=16] {'col'}, dimensions={0} | all-to-all | bytes 2097152 | tf_op jit(solution)/shard_map/all_to_all | solution.py:32
  536.8 3.5 reshape.18
  540.3 6.9 %copy.58 = bf16[2,16,32,16,32]{2,3,4,0,1:T(8,128)(2,1)} copy(bf16[2,16,32,16,32]{2,1,0,4,3:T(8,128)(2,1)} %bitcast.50) | data formatting | bytes 2097152 | tf_op jit(solution)/shard_map/all_to_all | solution.py:32
  547.2 0.0 copy-start
  547.2 6.1 reshape.11
  553.3 0.0 copy-done
  553.3 2.3 bitcast_convert_fusion
  555.6 7.2 %copy.20 = bf16[2,512,16,32]{3,2,0,1:T(8,128)(2,1)} copy(bf16[2,512,16,32]{1,3,2,0:T(8,128)(2,1)} %bitcast_convert_fusion) | data formatting | bytes 2097152 | tf_op jit(solution)/shard_map/convert_element_type | solution.py:35
  562.8 6.7 %reshape.19 = bf16[32,2,8192]{2,1,0:T(2,128)(2,1)S(1)} reshape(bf16[512,2,16,32]{3,2,1,0:T(8,128)(2,1)} %bitcast.49) | data formatting | bytes 2097152
  569.4 59.2 %all_to_all.37 = bf16[32,2,8192]{2,1,0:T(2,128)(2,1)S(1)} all-to-all(bf16[32,2,8192]{2,1,0:T(2,128)(2,1)S(1)} %reshape.19), channel_id=1, replica_groups=mesh['row'=32,'col'=16] {'row'}, dimensions={0} | all-to-all | bytes 2097152 | tf_op jit(solution)/shard_map/all_to_all | solution.py:39
  628.7 3.5 reshape.20
  632.2 0.0 copy-start.1
  632.2 3.5 copy.22
  635.7 0.0 copy-done.1
  635.7 2.8 fusion.2
Async XLA Ops:
  6.5 485.6 %all-reduce.2.cloned.1.call-start = ((), (), s32[]{:S(2)}) async-start(), calls=%async_computation.2 | async-start | bytes 2097152 | tf_op jit(solution)/shard_map/psum | solution.py:9
  494.9 2.8 copy-start.2
  547.2 6.1 copy-start
  632.2 3.5 copy-start.1
Sparse Core Ops, SparseCore 0:
  12.8 479.3 all-reduce.1
where the time goes:
time: 650 us; the launch traced here: 645 us
  waiting for transfers between devices  484 us (74%)
  blocking collectives  82.4 us (13%)
  local copies, waits for them, and re-layouts  54.4 us (8%)
  between operations  14.1 us (2%)
  matrix products  7.93 us (1%)
    psum x1, waiting for transfers between devices, broadcast(): return lax.psum(block, axis)  484 us
    all_to_all x1, blocking collectives, per_device(): lax.all_to_all(second, 'row', split_axis=1, concat_axis=2, tiled=True)  59.2 us
    all_to_all x1, blocking collectives, per_device(): lax.all_to_all(first, 'col', split_axis=3, concat_axis=2, tiled=True)  23.2 us
    unnamed x10, local copies, waits for them, and re-layouts  20.3 us
  transfers between devices with their start and end apart: 1, of which 1 were waited for; matrix products, arithmetic and copies ran while one was open for 0% of the time, Pallas kernels for 0%

commit v1 on v0

v1 whole, which is shorter than its diff:
```python
import functools

import jax
import jax.numpy as jnp
from jax import lax
from jax.experimental import pallas as pl
from jax.experimental.pallas import tpu as pltpu
from jax.sharding import PartitionSpec as P

MESH = pl.DeviceIdType.MESH
F32 = jnp.float32
BF16 = jnp.bfloat16
NT = (((1,), (1,)), ((), ()))


def butterfly(arrs, group):
    arrs = list(arrs)
    lane = lax.broadcasted_iota(jnp.int32, arrs[0].shape, 1)
    bit = 1
    while bit < len(arrs):
        shift = group * bit
        high = (lane & shift) != 0
        for a in range(len(arrs)):
            if a & bit:
                continue
            lo, hi = arrs[a], arrs[a | bit]
            arrs[a] = jnp.where(high, pltpu.roll(hi, shift, 1), lo)
            arrs[a | bit] = jnp.where(high, hi, pltpu.roll(lo, 128 - shift, 1))
        bit *= 2
    return arrs


def kernel(
    own_ref, e_ref, p_ref, out_ref,
    pb, mine, half, rb, cbuf, zb, dbuf, zg, qbuf, pp, m2, m3, x1, y1, r1, x2, sb, r2, x3, acc,
    pair_s, pair_r, plane_s, plane_r, zgrp_s, zgrp_r, zall_s, zall_r, gath_s, gath_r, back_s, back_r,
    local_sem, load_sem, col_s, col_r, row_s, row_r, out_sem,
):
    row = lax.axis_index("row")
    col = lax.axis_index("col")
    x_lo, z = row // 16, row % 16
    core, xy = col % 2, col // 2
    chip = x_lo * 8 + xy
    member, zgroup = z % 4, z // 4

    def at_chip(c):
        return ((c // 8) * 16 + z, (c % 8) * 2 + core)

    load_own = pltpu.make_async_copy(p_ref.at[core], mine, local_sem)
    load_own.start()
    for r in range(2):
        pltpu.make_async_copy(e_ref.at[r], x1.at[:, pl.ds(r * 512, 512)], load_sem).start()

    barrier = pltpu.get_barrier_semaphore()

    def greet(dev):
        pl.semaphore_signal(barrier, inc=1, device_id=dev, device_id_type=MESH)

    def greet_plane(d, _):
        greet(at_chip((chip + d) % 16))
        return 0

    def greet_other(d, _):
        greet((row, d * 2 + 1 - core))
        return 0

    def greet_row(d, _):
        for x in range(2):
            greet((x * 16 + (z + d) % 16, col))
        return 0

    lax.fori_loop(1, 16, greet_row, 0)
    lax.fori_loop(1, 16, greet_plane, 0)
    lax.fori_loop(0, 8, greet_other, 0)
    pl.semaphore_wait(barrier, 53)

    def send(src, dst, ssem, rsem, dev):
        pltpu.make_async_remote_copy(
            src_ref=src, dst_ref=dst, send_sem=ssem, recv_sem=rsem,
            device_id=dev, device_id_type=MESH,
        ).start()

    def wait_bytes(ref, sem):
        pltpu.make_async_copy(ref, ref, sem).wait()

    send(p_ref.at[1 - core], pb, pair_s, pair_r, (row, xy * 2 + 1 - core))
    load_own.wait()
    wait_bytes(pb, pair_r)
    from_me = own_ref[0] == core

    def pick(n, _):
        rows = pl.ds(pl.multiple_of(n * 32, 32), 32)
        half[rows, :] = jnp.where(from_me, mine[rows, :].astype(F32), pb[rows, :].astype(F32)).astype(BF16)
        return 0

    lax.fori_loop(0, 16, pick, 0)

    def rows32(n):
        return pl.ds(pl.multiple_of(n * 32, 32), 32)

    def scatter_plane(d, _):
        c = (chip + d) % 16
        send(half.at[rows32(c), :], rb.at[chip], plane_s, plane_r, at_chip(c))
        return 0

    lax.fori_loop(1, 16, scatter_plane, 0)
    pltpu.make_async_copy(half.at[rows32(chip), :], rb.at[chip], plane_r).start()
    wait_bytes(rb, plane_r)
    cbuf[...] = rb[own_ref[1]]

    def lanes128(n):
        return pl.ds(pl.multiple_of(n * 128, 128), 128)

    def scatter_z(d, _):
        m = (member + d) % 4
        send(cbuf.at[:, lanes128(m)], zb.at[member], zgrp_s, zgrp_r, (x_lo * 16 + zgroup * 4 + m, col))
        return 0

    lax.fori_loop(1, 4, scatter_z, 0)
    pltpu.make_async_copy(cbuf.at[:, lanes128(member)], zb.at[member], zgrp_r).start()
    wait_bytes(zb, zgrp_r)
    dbuf[...] = zb[own_ref[2]]

    def gather_z(d, _):
        dz = 8 + jnp.where(d % 2 == 0, d // 2, -((d + 1) // 2))
        send(dbuf, zg.at[z], zall_s, zall_r, (x_lo * 16 + (z + dz) % 16, col))
        return 0

    lax.fori_loop(0, 15, gather_z, 0)
    pltpu.make_async_copy(dbuf, zg.at[z], zall_r).start()
    wait_bytes(zg, zall_r)
    for m in range(4):
        qbuf[:, m * 128 : (m + 1) * 128] = zg[own_ref[3] * 4 + m]

    def gather_plane(d, _):
        c = (chip + d) % 16
        send(qbuf, pp.at[core, rows32(chip), :], gath_s, gath_r.at[chip], at_chip(c))
        return 0

    lax.fori_loop(1, 16, gather_plane, 0)
    pltpu.make_async_copy(qbuf, pp.at[core, rows32(chip), :], gath_r.at[chip]).start()

    def gather_pair(d, _):
        c = (chip + d) % 16
        part = pp.at[core, rows32(c), :]
        wait_bytes(part, gath_r.at[c])
        send(part, part, back_s, back_r, (row, xy * 2 + 1 - core))
        return 0

    lax.fori_loop(0, 16, gather_pair, 0)
    wait_bytes(pb, back_r)

    def build(n, _):
        rows = rows32(n)
        low = pl.ds(pl.multiple_of(512 + n * 32, 32), 32)
        re, im = pp[0, rows, :], pp[1, rows, :]
        m2[rows, 0:512] = re
        m2[rows, 512:1024] = -im
        m2[low, 0:512] = im
        m2[low, 512:1024] = re
        return 0

    lax.fori_loop(0, 16, build, 0)
    wait_bytes(x1, load_sem)

    for h in range(2):
        def contract_k(n, _, h=h):
            rows = pl.ds(pl.multiple_of(n * 256, 256), 256)
            y = lax.dot_general(m2[rows, :], x1[h * 256 : (h + 1) * 256, :], NT, preferred_element_type=F32)
            y1[h, n // 2, pl.ds(pl.multiple_of((n % 2) * 256, 256), 256), :] = y.astype(BF16)
            return 0

        lax.fori_loop(0, 4, contract_k, 0)

        for ch in range(2):
            q = h * 2 + ch

            def part(c, h=h, ch=ch):
                return y1.at[h, :, pl.ds(pl.multiple_of(c * 32 + ch * 16, 16), 16), :]

            def scatter_col(d, _, q=q, part=part):
                c = (col + d) % 16
                send(part(c), r1.at[q, col], col_s.at[q], col_r.at[q], (row, c))
                return 0

            lax.fori_loop(1, 16, scatter_col, 0)
            pltpu.make_async_copy(part(col), r1.at[q, col], col_r.at[q]).start()

    def second_step(q, _):
        wait_bytes(r1.at[q], col_r.at[q])

        def swap_in(n, _):
            r, chi = n // 4, n % 4
            for ib in range(2):
                got = [r1[q, chi * 4 + k, r, :, ib * 128 : (ib + 1) * 128].astype(F32) for k in range(4)]
                for k, v in enumerate(butterfly(got, 32)):
                    x2[(ib * 4 + k) * 16 : (ib * 4 + k + 1) * 16, lanes128(n)] = v.astype(BF16)
            return 0

        lax.fori_loop(0, 8, swap_in, 0)

        def contract_j(n, _):
            rows = pl.ds(pl.multiple_of(n * 128, 128), 128)
            y = lax.dot_general(x2[...], m2[rows, :], NT, preferred_element_type=F32)
            s, hi = n // 4, n % 4
            got = [y[k * 16 : (k + 1) * 16, :] for k in range(8)]
            for k, v in enumerate(butterfly(got, 16)):
                sb[q, hi * 8 + k, s, :, :] = v.astype(BF16)
            return 0

        lax.fori_loop(0, 8, contract_j, 0)

        def scatter_row(d, _):
            dz = 8 + jnp.where(d % 2 == 0, d // 2, -((d + 1) // 2))
            for dx in range(2):
                to = ((x_lo + dx) % 2) * 16 + (z + dz) % 16
                send(sb.at[q, to], r2.at[q, row], row_s.at[q], row_r.at[q], (to, col))
            return 0

        lax.fori_loop(0, 15, scatter_row, 0)
        to = (1 - x_lo) * 16 + z
        send(sb.at[q, to], r2.at[q, row], row_s.at[q], row_r.at[q], (to, col))
        pltpu.make_async_copy(sb.at[q, row], r2.at[q, row], row_r.at[q]).start()
        return 0

    lax.fori_loop(0, 4, second_step, 0)

    a = lax.broadcasted_iota(jnp.int32, (256, 128), 0)
    b = lax.broadcasted_iota(jnp.int32, (256, 128), 1)
    for h in range(2):
        perm = (a == (b % 16) * 16 + h * 8 + b // 16).astype(F32).astype(BF16)

        def permute(n, _, h=h, perm=perm):
            rows = pl.ds(pl.multiple_of(n * 256, 256), 256)
            for k in range(4):
                v = jnp.dot(m2[rows, k * 256 : (k + 1) * 256], perm, preferred_element_type=F32)
                m3[h, rows, k * 128 : (k + 1) * 128] = v.astype(BF16)
            return 0

        lax.fori_loop(0, 4, permute, 0)

    def third_step(q, first):
        h, ch = q // 2, q % 2
        wait_bytes(r2.at[q], row_r.at[q])

        def swap_out(n, _):
            r, x = n // 2, n % 2
            got = [r2[q, x * 16 + k, r, :, :].astype(F32) for k in range(16)]
            for k, v in enumerate(butterfly(got, 1)):
                x3[k * 16 : (k + 1) * 16, lanes128(n)] = v.astype(BF16)
            return 0

        lax.fori_loop(0, 4, swap_out, 0)

        def contract_i(n, _):
            rows = pl.ds(pl.multiple_of(n * 256, 256), 256)
            s = n // 2
            lanes = pl.ds(pl.multiple_of((n % 2) * 256, 256), 256)
            y = lax.dot_general(x3[...], m3[h, rows, :], NT, preferred_element_type=F32)
            y = y.reshape(16, 16, 256)
            if first:
                acc[ch, s, :, :, lanes] = y
            else:
                acc[ch, s, :, :, lanes] += y
            return 0

        lax.fori_loop(0, 4, contract_i, 0)

    for q in range(2):
        third_step(q, True)
    for q in range(2, 4):
        third_step(q, False)
        ch = q % 2
        pltpu.make_async_copy(acc.at[ch], out_ref.at[:, :, pl.ds(ch * 16, 16), :], out_sem).start()

    wait_bytes(pb, pair_s)
    wait_bytes(rb.at[pl.ds(0, 15)], plane_s)
    wait_bytes(zb.at[pl.ds(0, 3)], zgrp_s)
    wait_bytes(zg.at[pl.ds(0, 15)], zall_s)
    wait_bytes(rb.at[pl.ds(0, 15)], gath_s)
    wait_bytes(pb, back_s)
    for q in range(4):
        wait_bytes(r1.at[q, pl.ds(0, 15)], col_s.at[q])
        wait_bytes(r2.at[q, pl.ds(0, 31)], row_s.at[q])
    wait_bytes(acc, out_sem)


def per_device(elemental, perambulators, source_owner):
    owner = source_owner[0]
    row, col = owner // 16, owner % 16
    own = jnp.stack([col % 2, (row // 16) * 8 + col // 2, row % 4, (row % 16) // 4]).astype(jnp.int32)
    dma = pltpu.SemaphoreType.DMA
    vmem = pltpu.VMEM
    out = pl.pallas_call(
        kernel,
        out_shape=jax.ShapeDtypeStruct((2, 16, 32, 512), F32),
        in_specs=[
            pl.BlockSpec(memory_space=pltpu.SMEM),
            pl.BlockSpec(memory_space=pl.ANY),
            pl.BlockSpec(memory_space=pl.ANY),
        ],
        out_specs=pl.BlockSpec(memory_space=pl.ANY),
        scratch_shapes=[
            vmem((512, 512), BF16),
            vmem((512, 512), BF16),
            vmem((512, 512), BF16),
            vmem((16, 32, 512), BF16),
            vmem((32, 512), BF16),
            vmem((4, 32, 128), BF16),
            vmem((32, 128), BF16),
            vmem((16, 32, 128), BF16),
            vmem((32, 512), BF16),
            vmem((2, 512, 512), BF16),
            vmem((1024, 1024), BF16),
            vmem((2, 1024, 512), BF16),
            vmem((512, 1024), BF16),
            vmem((2, 2, 512, 256), BF16),
            vmem((4, 16, 2, 16, 256), BF16),
            vmem((128, 1024), BF16),
            vmem((4, 32, 2, 16, 128), BF16),
            vmem((4, 32, 2, 16, 128), BF16),
            vmem((256, 512), BF16),
            vmem((2, 2, 16, 16, 512), F32),
            dma, dma, dma, dma, dma, dma, dma, dma, dma, dma((16,)), dma, dma,
            dma, dma, dma((4,)), dma((4,)), dma((4,)), dma((4,)), dma,
        ],
        compiler_params=pltpu.CompilerParams(collective_id=0, has_side_effects=True),
    )(own, elemental.reshape(2, 512, 512), perambulators[0])
    return out.transpose(0, 3, 1, 2)


def solution(mesh):
    in_specs = (P(None, "row", "col", None), P(("row", "col"), None, None, None), P())
    out_specs = P(None, None, "row", "col")
    return jax.shard_map(
        per_device, mesh=mesh, in_specs=in_specs, out_specs=out_specs, check_vma=False
    )
```

time: 650 us -> 120 us (0.18)
  waiting for transfers between devices: 484 us -> 0 us
  Pallas kernels: 0 us -> 115 us
  blocking collectives: 82.4 us -> 0 us
  local copies, waits for them, and re-layouts: 54.4 us -> 3.19 us
  between operations: 14.1 us -> 0.77 us
  matrix products: 7.93 us -> 0 us
    psum x1 -> x0, waiting for transfers between devices: 484 us -> none  [broadcast(): return lax.psum(block, axis)]
    pallas_call x0 -> x1, Pallas kernels: none -> 115 us  [per_device(): pl.pallas_call(kernel, out_shape=jax.ShapeDtypeStruct((2, 16, 32, 512), F...]
    all_to_all x2 -> x0, blocking collectives: 82.4 us -> none  [the longest x1 59.2 us: per_device(): lax.all_to_all(second, 'row', split_axis=1, concat_axis=2, tiled=True)]
    unnamed x10 -> x1, local copies, waits for them, and re-layouts: 20.3 us -> 3.19 us
    all_to_all x3 -> x0, local copies, waits for them, and re-layouts: 16.4 us -> none  [the longest x2 12.9 us: per_device(): lax.all_to_all(first, 'col', split_axis=3, concat_axis=2, tiled=True)]
    convert_element_type x2 -> x0, local copies, waits for them, and re-layouts: 13.6 us -> none  [the longest x1 7.2 us: per_device(): second = result.astype(jnp.bfloat16)]
    dot_general x3 -> x0, matrix products: 7.93 us -> none  [the longest x1 2.88 us: per_device(): jnp.einsum('scrk,rijk->sijc', mixing, elemental, preferred_element_type=j...]
  transfers between devices with their start and end apart: 1 -> 0, of which waited for: 1 -> 0; matrix products, arithmetic and copies ran while one was open for 0% -> 0% of each run, Pallas kernels for 0% -> 0%
where the time goes in v1:
time: 120 us
  Pallas kernels  115 us (96%)
  local copies, waits for them, and re-layouts  3.19 us (3%)
    pallas_call x1, Pallas kernels, per_device(): pl.pallas_call(kernel, out_shape=jax.ShapeDtypeStruct((2, 16, 32, 512), F...  115 us
    unnamed x1, local copies, waits for them, and re-layouts  3.19 us

profile of v1, /device:TPU:1, one launch (start us, length us, event | category | flops | bytes accessed | tf_op | source)
XLA Modules:
  0.0 119.8 jit_solution(10128517182817747199)
XLA Ops:
  0.8 0.6 pad_add_fusion.own_ref
  1.4 115.2 %shard_map.37 = f32[2,16,32,512]{3,2,1,0:T(8,128)} custom-call(s32[4]{0:T(128)} %pad_add_fusion.own_ref, bf16[2,512,512]{2,1,0:T(8,128)(2,1)} %bitcast.13, bf16[2,512,512]{2,1,0:T(8,128)(2,1)} %bitcast.14), custom_call_target="tpu_custom_call" | custom-call | tf_op jit(solution)/shard_map/pallas_call | solution.py:294
  116.6 3.2 %copy.6 = f32[2,512,16,32]{1,3,2,0:T(8,128)} copy(f32[2,512,16,32]{1,3,2,0:T(8,128)} %bitcast.12) | data formatting | bytes 4194304

commit v2 on v1

v2 whole, which is shorter than its diff:
```python
import functools

import jax
import jax.numpy as jnp
from jax import lax
from jax.experimental import pallas as pl
from jax.experimental.pallas import tpu as pltpu
from jax.sharding import PartitionSpec as P

MESH = pl.DeviceIdType.MESH
F32 = jnp.float32
BF16 = jnp.bfloat16
NT = (((1,), (1,)), ((), ()))
FAR_FIRST = sorted(
    ((dx, dy) for dx in range(4) for dy in range(4) if dx or dy),
    key=lambda d: -(min(d[0], 4 - d[0]) + min(d[1], 4 - d[1])),
)


def butterfly(arrs, group):
    arrs = list(arrs)
    lane = lax.broadcasted_iota(jnp.int32, arrs[0].shape, 1)
    bit = 1
    while bit < len(arrs):
        shift = group * bit
        high = (lane & shift) != 0
        for a in range(len(arrs)):
            if a & bit:
                continue
            lo, hi = arrs[a], arrs[a | bit]
            arrs[a] = jnp.where(high, pltpu.roll(hi, shift, 1), lo)
            arrs[a | bit] = jnp.where(high, hi, pltpu.roll(lo, 128 - shift, 1))
        bit *= 2
    return arrs


def kernel(
    own_ref, e_ref, p_ref, acc, x3, m3b,
    pb, mine, half, rb, cbuf, zb, dbuf, zg, qbuf, pp, m2, m3a, x1, y1, r1, x2, sb, r2,
    pair_s, pair_r, plane_s, plane_r, zgrp_s, zgrp_r, zall_s, zall_r, gath_s, gath_r, back_s, back_r,
    local_sem, load_sem, col_s, col_r, row_s, row_r,
):
    row = lax.axis_index("row")
    col = lax.axis_index("col")
    x_lo, z = row // 16, row % 16
    core, xy = col % 2, col // 2
    chip = x_lo * 8 + xy
    member, zgroup = z % 4, z // 4
    zhalf, zrest = z // 8, z % 8
    x_hi, y = xy // 4, xy % 4
    x = x_hi * 2 + x_lo
    other = (row, xy * 2 + 1 - core)

    def in_plane(dx, dy):
        px, py = (x + dx) % 4, (y + dy) % 4
        to = (px // 2) * 4 + py
        return (px % 2) * 8 + to, ((px % 2) * 16 + z, to * 2 + core)

    barrier = pltpu.get_barrier_semaphore()

    def greet(dev):
        pl.semaphore_signal(barrier, inc=1, device_id=dev, device_id_type=MESH)

    def greet_other(d, _):
        greet((row, d * 2 + 1 - core))
        return 0

    def greet_row(d, _):
        for x in range(2):
            greet((x * 16 + (z + d) % 16, col))
        return 0

    lax.fori_loop(1, 16, greet_row, 0)
    for step in FAR_FIRST:
        greet(in_plane(*step)[1])
    lax.fori_loop(0, 8, greet_other, 0)

    load_own = pltpu.make_async_copy(p_ref.at[core], mine, local_sem)
    load_own.start()
    for r in range(2):
        pltpu.make_async_copy(e_ref.at[r], x1.at[:, pl.ds(r * 512, 512)], load_sem).start()
    pl.semaphore_wait(barrier, 53)

    def send(src, dst, ssem, rsem, dev):
        pltpu.make_async_remote_copy(
            src_ref=src, dst_ref=dst, send_sem=ssem, recv_sem=rsem,
            device_id=dev, device_id_type=MESH,
        ).start()

    def wait_bytes(ref, sem):
        pltpu.make_async_copy(ref, ref, sem).wait()

    send(p_ref.at[1 - core], pb, pair_s, pair_r, other)
    load_own.wait()
    wait_bytes(pb, pair_r)
    owner = own_ref[0]
    owner_row, owner_col = lax.div(owner, 16), lax.rem(owner, 16)
    from_me = lax.rem(owner_col, 2) == core
    owner_chip = lax.div(owner_row, 16) * 8 + lax.div(owner_col, 2)
    owner_z = lax.rem(owner_row, 16)

    def pick(n, _):
        rows = pl.ds(pl.multiple_of(n * 32, 32), 32)
        half[rows, :] = jnp.where(from_me, mine[rows, :], pb[rows, :])
        return 0

    lax.fori_loop(0, 16, pick, 0)

    def rows32(n):
        return pl.ds(pl.multiple_of(n * 32, 32), 32)

    for step in FAR_FIRST:
        c, to = in_plane(*step)
        send(half.at[rows32(c), :], rb.at[chip], plane_s, plane_r, to)
    pltpu.make_async_copy(half.at[rows32(chip), :], rb.at[chip], plane_r).start()
    wait_bytes(rb, plane_r)
    cbuf[...] = rb[owner_chip]

    def lanes128(n):
        return pl.ds(pl.multiple_of(n * 128, 128), 128)

    def scatter_z(d, _):
        m = (member + d) % 4
        send(cbuf.at[:, lanes128(m)], zb.at[member], zgrp_s, zgrp_r, (x_lo * 16 + zgroup * 4 + m, col))
        return 0

    lax.fori_loop(1, 4, scatter_z, 0)
    pltpu.make_async_copy(cbuf.at[:, lanes128(member)], zb.at[member], zgrp_r).start()
    wait_bytes(zb, zgrp_r)
    dbuf[...] = zb[lax.rem(owner_z, 4)]

    def gather_z(d, _):
        dz = 8 + jnp.where(d % 2 == 0, d // 2, -((d + 1) // 2))
        send(dbuf, zg.at[z], zall_s, zall_r, (x_lo * 16 + (z + dz) % 16, col))
        return 0

    lax.fori_loop(0, 15, gather_z, 0)
    pltpu.make_async_copy(dbuf, zg.at[z], zall_r).start()
    wait_bytes(zg, zall_r)
    for m in range(4):
        qbuf[:, m * 128 : (m + 1) * 128] = zg[lax.div(owner_z, 4) * 4 + m]

    for step in FAR_FIRST:
        send(qbuf, pp.at[core, rows32(chip), :], gath_s, gath_r.at[chip], in_plane(*step)[1])
    pltpu.make_async_copy(qbuf, pp.at[core, rows32(chip), :], gath_r.at[chip]).start()
    for step in ((0, 0), *FAR_FIRST):
        c = in_plane(*step)[0]
        part = pp.at[core, rows32(c), :]
        wait_bytes(part, gath_r.at[c])
        send(part, part, back_s, back_r, other)
    wait_bytes(pb, back_r)

    def build(n, _):
        re, im = pp[0, rows32(n), :].reshape(2, 16, 512), pp[1, rows32(n), :].reshape(2, 16, 512)
        m2[0, n, :, :, 0:512] = re
        m2[0, n, :, :, 512:1024] = -im
        m2[1, n, :, :, 0:512] = im
        m2[1, n, :, :, 512:1024] = re
        return 0

    lax.fori_loop(0, 16, build, 0)
    wait_bytes(x1, load_sem)

    def contract_k(q):
        h, ch = q // 2, q % 2
        for s in range(2):
            y = lax.dot_general(
                m2[s, :, ch].reshape(256, 1024), x1[h * 256 : (h + 1) * 256, :], NT, preferred_element_type=F32
            )
            y1[q, s] = y.astype(BF16)

    def exchange_col(q):
        def scatter_col(n, _):
            k = n % 8
            dy = jnp.where(k // 2 == 0, 2, jnp.where(k // 2 == 1, 1, jnp.where(k // 2 == 2, 3, 0)))
            c = (((x_hi + 1 - n // 8) % 2) * 4 + (y + dy) % 4) * 2 + (core + 1 - k % 2) % 2
            rows = pl.ds(pl.multiple_of(c * 16, 16), 16)
            send(y1.at[q, :, rows, :], r1.at[q, col], col_s.at[q], col_r.at[q, col // 4], (row, c))
            return 0

        lax.fori_loop(0, 15, scatter_col, 0)
        rows = pl.ds(pl.multiple_of(col * 16, 16), 16)
        pltpu.make_async_copy(y1.at[q, :, rows, :], r1.at[q, col], col_r.at[q, col // 4]).start()

    def contract_j(q):
        def swap_in(n, _):
            chi = (col // 4 + n) % 4
            wait_bytes(r1.at[q, pl.ds(chi * 4, 4)], col_r.at[q, chi])
            for r in range(2):
                for ib in range(2):
                    got = [r1[q, chi * 4 + k, r, :, ib * 128 : (ib + 1) * 128] for k in range(4)]
                    for k, v in enumerate(butterfly(got, 32)):
                        x2[(ib * 4 + k) * 16 : (ib * 4 + k + 1) * 16, lanes128(r * 4 + chi)] = v
            return 0

        lax.fori_loop(0, 4, swap_in, 0)

        for dx, dz in ((1, 1), (0, 1), (1, 0), (0, 0)):
            to_x, to_half = (x_lo + dx) % 2, (zhalf + dz) % 2
            hi = to_x * 2 + to_half
            y = lax.dot_general(
                x2[...], m2[:, pl.ds(hi * 4, 4)].reshape(256, 1024), NT, preferred_element_type=F32
            ).astype(BF16)
            for s in range(2):
                got = [y[k * 16 : (k + 1) * 16, s * 128 : (s + 1) * 128] for k in range(8)]
                for k, v in enumerate(butterfly(got, 16)):
                    sb[q, hi * 8 + k, s, :, :] = v

            def scatter_row(d, _):
                to = to_x * 16 + to_half * 8 + (zrest + d) % 8
                send(sb.at[q, to], r2.at[q, row], row_s.at[q], row_r.at[q], (to, col))
                return 0

            lax.fori_loop(0 if dx or dz else 1, 8, scatter_row, 0)
        pltpu.make_async_copy(sb.at[q, row], r2.at[q, row], row_r.at[q]).start()

    contract_k(0)
    exchange_col(0)
    for q in (1, 2, 3):
        contract_k(q)
    exchange_col(1)
    contract_j(0)
    exchange_col(2)
    contract_j(1)
    exchange_col(3)
    contract_j(2)
    contract_j(3)

    a = lax.broadcasted_iota(jnp.int32, (256, 128), 0)
    b = lax.broadcasted_iota(jnp.int32, (256, 128), 1)
    for h in range(2):
        perm = (a == (b % 16) * 16 + h * 8 + b // 16).astype(F32).astype(BF16)

        m3 = (m3a, m3b)[h]

        def permute(n, _, m3=m3, perm=perm):
            block = m2[n // 2, pl.ds((n % 2) * 8, 8)].reshape(256, 1024)
            rows = pl.ds(pl.multiple_of(n * 256, 256), 256)
            for k in range(4):
                v = jnp.dot(block[:, k * 256 : (k + 1) * 256], perm, preferred_element_type=F32)
                m3[rows, k * 128 : (k + 1) * 128] = v.astype(BF16)
            return 0

        lax.fori_loop(0, 4, permute, 0)

    for q in range(4):
        ch = q % 2
        wait_bytes(r2.at[q], row_r.at[q])

        def swap_out(n, _, q=q):
            r, x = n // 2, n % 2
            got = [r2[q, x * 16 + k, r, :, :] for k in range(16)]
            for k, v in enumerate(butterfly(got, 1)):
                x3[k * 16 : (k + 1) * 16, lanes128(n)] = v
            return 0

        lax.fori_loop(0, 4, swap_out, 0)
        if q == 3:
            break
        m3 = (m3a, m3b)[q // 2]

        def contract_i(n, _, q=q, ch=ch, m3=m3):
            rows = pl.ds(pl.multiple_of(n * 256, 256), 256)
            lanes = pl.ds(pl.multiple_of((n % 2) * 256, 256), 256)
            v = lax.dot_general(x3[...], m3[rows, :], NT, preferred_element_type=F32).reshape(16, 16, 256)
            if q < 2:
                acc[ch, n // 2, :, :, lanes] = v
            else:
                acc[ch, n // 2, :, :, lanes] += v
            return 0

        lax.fori_loop(0, 4, contract_i, 0)

    wait_bytes(pb, pair_s)
    wait_bytes(rb.at[pl.ds(0, 15)], plane_s)
    wait_bytes(zb.at[pl.ds(0, 3)], zgrp_s)
    wait_bytes(zg.at[pl.ds(0, 15)], zall_s)
    wait_bytes(rb.at[pl.ds(0, 15)], gath_s)
    wait_bytes(pb, back_s)
    for q in range(4):
        wait_bytes(r1.at[q, pl.ds(0, 15)], col_s.at[q])
        wait_bytes(r2.at[q, pl.ds(0, 31)], row_s.at[q])


def finish(acc, x3, m3, out_ref, last, sem):
    done = pltpu.make_async_copy(acc.at[0], out_ref.at[:, :, pl.ds(0, 16), :], sem.at[2])
    done.start()
    copies = []
    for s in range(2):
        for lane in range(0, 512, 256):
            v = lax.dot_general(
                x3[...], m3[s * 512 + lane : s * 512 + lane + 256, :], NT, preferred_element_type=F32
            )
            last[s, :, :, lane : lane + 256] = acc[1, s, :, :, lane : lane + 256] + v.reshape(16, 16, 256)
        copies.append(pltpu.make_async_copy(last.at[s], out_ref.at[s, :, pl.ds(16, 16), :], sem.at[s]))
        copies[-1].start()
    for copy in (done, *copies):
        copy.wait()


def per_device(elemental, perambulators, source_owner):
    dma = pltpu.SemaphoreType.DMA
    vmem = pltpu.VMEM
    held = pl.BlockSpec(memory_space=pltpu.VMEM)
    parts = pl.pallas_call(
        kernel,
        out_shape=(vmem((2, 2, 16, 16, 512), F32), vmem((256, 512), BF16), vmem((1024, 512), BF16)),
        in_specs=[
            pl.BlockSpec(memory_space=pltpu.SMEM),
            pl.BlockSpec(memory_space=pltpu.HBM),
            pl.BlockSpec(memory_space=pltpu.HBM),
        ],
        out_specs=(held, held, held),
        scratch_shapes=[
            vmem((512, 512), BF16),
            vmem((512, 512), BF16),
            vmem((512, 512), BF16),
            vmem((16, 32, 512), BF16),
            vmem((32, 512), BF16),
            vmem((4, 32, 128), BF16),
            vmem((32, 128), BF16),
            vmem((16, 32, 128), BF16),
            vmem((32, 512), BF16),
            vmem((2, 512, 512), BF16),
            vmem((2, 16, 2, 16, 1024), BF16),
            vmem((1024, 512), BF16),
            vmem((512, 1024), BF16),
            vmem((4, 2, 256, 256), BF16),
            vmem((4, 16, 2, 16, 256), BF16),
            vmem((128, 1024), BF16),
            vmem((4, 32, 2, 16, 128), BF16),
            vmem((4, 32, 2, 16, 128), BF16),
            dma, dma, dma, dma, dma, dma, dma, dma, dma, dma((16,)), dma, dma,
            dma, dma, dma((4,)), dma((4, 4)), dma((4,)), dma((4,)),
        ],
        compiler_params=pltpu.CompilerParams(collective_id=0, has_side_effects=True, vmem_limit_bytes=60 << 20),
    )(source_owner, elemental.reshape(2, 512, 512), perambulators[0])
    out = pl.pallas_call(
        finish,
        out_shape=jax.ShapeDtypeStruct((2, 16, 32, 512), F32),
        in_specs=[held, held, held],
        out_specs=pl.BlockSpec(memory_space=pltpu.HBM),
        scratch_shapes=[vmem((2, 16, 16, 512), F32), dma((3,))],
        compiler_params=pltpu.CompilerParams(vmem_limit_bytes=12 << 20),
    )(*parts)
    return out.transpose(0, 3, 1, 2)


def solution(mesh):
    in_specs = (P(None, "row", "col", None), P(("row", "col"), None, None, None), P())
    out_specs = P(None, None, "row", "col")
    return jax.shard_map(
        per_device, mesh=mesh, in_specs=in_specs, out_specs=out_specs, check_vma=False
    )
```

time: 120 us -> 108 us (0.900); the launches traced: 120 us -> 106 us
  Pallas kernels: 115 us -> 106 us
  local copies, waits for them, and re-layouts: 3.19 us -> 0 us
    pallas_call x1 -> x2, Pallas kernels: 115 us -> 106 us  [the longest x1 104 us: per_device(): pl.pallas_call(kernel, out_shape=(vmem((2, 2, 16, 16, 512), F32), vmem((2...]
    unnamed x1 -> x0, local copies, waits for them, and re-layouts: 3.19 us -> none
where the time goes in v2:
time: 108 us; the launch traced here: 106 us
  Pallas kernels  106 us (98%)
    pallas_call x1, Pallas kernels, per_device(): pl.pallas_call(kernel, out_shape=(vmem((2, 2, 16, 16, 512), F32), vmem((2...  104 us

profile of v2, /device:TPU:1, one launch (start us, length us, event | category | flops | bytes accessed | tf_op | source)
XLA Modules:
  0.0 106.3 jit_solution(4352856972870332177)
XLA Ops:
  0.7 104.1 %shard_map.37 = (f32[2,2,16,16,512]{4,3,2,1,0:T(8,128)S(1)}, bf16[256,512]{1,0:T(8,128)(2,1)S(1)}, bf16[1024,512]{1,0:T(8,128)(2,1)S(1)}) custom-call(s32[1]{0:T(128)S(6)} %copy.4.own_ref, bf16[2,512,512]{2,1,0:T(8,128)(2,1)} %bitcast.3, bf16[2,512,512]{2,1,0:T(8,128)(2,1)} %bitcast.4), custom_call_target="tpu_custom_call" | custom-call | tf_op jit(solution)/shard_map/pallas_call | solution.py:305
  104.7 1.6 %shard_map.38 = f32[2,16,32,512]{3,2,1,0:T(8,128)} custom-call(f32[2,2,16,16,512]{4,3,2,1,0:T(8,128)S(1)} %get-tuple-element.8.acc, bf16[256,512]{1,0:T(8,128)(2,1)S(1)} %get-tuple-element.9.x3, bf16[1024,512]{1,0:T(8,128)(2,1)S(1)} %get-tuple-element.10.m3), custom_call_target="tpu_custom_call" | custom-call | tf_op jit(solution)/shard_map/pallas_call | solution.py:338

commit v3 on v2

--- a/solution.py
+++ b/solution.py
@@ -36,7 +36,7 @@
 
 def kernel(
     own_ref, e_ref, p_ref, acc, x3, m3b,
-    pb, mine, half, rb, cbuf, zb, dbuf, zg, qbuf, pp, m2, m3a, x1, y1, r1, x2, sb, r2,
+    pb, mine, half, rb0, rb1, cbuf, zb0, zb1, dbuf, zg0, zg1, qbuf, pp, m2, m3a, x1, y1, r1, x2, sb, r2,
     pair_s, pair_r, plane_s, plane_r, zgrp_s, zgrp_r, zall_s, zall_r, gath_s, gath_r, back_s, back_r,
     local_sem, load_sem, col_s, col_r, row_s, row_r,
 ):
@@ -48,6 +48,7 @@
     member, zgroup = z % 4, z // 4
     zhalf, zrest = z // 8, z % 8
     x_hi, y = xy // 4, xy % 4
+    rb, zb, zg = (rb0, rb1), (zb0, zb1), (zg0, zg1)
     x = x_hi * 2 + x_lo
     other = (row, xy * 2 + 1 - core)
 
@@ -75,8 +76,8 @@
         greet(in_plane(*step)[1])
     lax.fori_loop(0, 8, greet_other, 0)
 
-    load_own = pltpu.make_async_copy(p_ref.at[core], mine, local_sem)
-    load_own.start()
+    for t in range(2):
+        pltpu.make_async_copy(p_ref.at[core, :, t], mine.at[t], local_sem.at[t]).start()
     for r in range(2):
         pltpu.make_async_copy(e_ref.at[r], x1.at[:, pl.ds(r * 512, 512)], load_sem).start()
     pl.semaphore_wait(barrier, 53)
@@ -90,76 +91,80 @@
     def wait_bytes(ref, sem):
         pltpu.make_async_copy(ref, ref, sem).wait()
 
-    send(p_ref.at[1 - core], pb, pair_s, pair_r, other)
-    load_own.wait()
-    wait_bytes(pb, pair_r)
     owner = own_ref[0]
     owner_row, owner_col = lax.div(owner, 16), lax.rem(owner, 16)
     from_me = lax.rem(owner_col, 2) == core
     owner_chip = lax.div(owner_row, 16) * 8 + lax.div(owner_col, 2)
     owner_z = lax.rem(owner_row, 16)
 
-    def pick(n, _):
-        rows = pl.ds(pl.multiple_of(n * 32, 32), 32)
-        half[rows, :] = jnp.where(from_me, mine[rows, :], pb[rows, :])
-        return 0
-
-    lax.fori_loop(0, 16, pick, 0)
-
-    def rows32(n):
-        return pl.ds(pl.multiple_of(n * 32, 32), 32)
-
-    for step in FAR_FIRST:
-        c, to = in_plane(*step)
-        send(half.at[rows32(c), :], rb.at[chip], plane_s, plane_r, to)
-    pltpu.make_async_copy(half.at[rows32(chip), :], rb.at[chip], plane_r).start()
-    wait_bytes(rb, plane_r)
-    cbuf[...] = rb[owner_chip]
-
     def lanes128(n):
         return pl.ds(pl.multiple_of(n * 128, 128), 128)
 
-    def scatter_z(d, _):
-        m = (member + d) % 4
-        send(cbuf.at[:, lanes128(m)], zb.at[member], zgrp_s, zgrp_r, (x_lo * 16 + zgroup * 4 + m, col))
-        return 0
-
-    lax.fori_loop(1, 4, scatter_z, 0)
-    pltpu.make_async_copy(cbuf.at[:, lanes128(member)], zb.at[member], zgrp_r).start()
-    wait_bytes(zb, zgrp_r)
-    dbuf[...] = zb[lax.rem(owner_z, 4)]
-
-    def gather_z(d, _):
-        dz = 8 + jnp.where(d % 2 == 0, d // 2, -((d + 1) // 2))
-        send(dbuf, zg.at[z], zall_s, zall_r, (x_lo * 16 + (z + dz) % 16, col))
-        return 0
-
-    lax.fori_loop(0, 15, gather_z, 0)
-    pltpu.make_async_copy(dbuf, zg.at[z], zall_r).start()
-    wait_bytes(zg, zall_r)
-    for m in range(4):
-        qbuf[:, m * 128 : (m + 1) * 128] = zg[lax.div(owner_z, 4) * 4 + m]
-
-    for step in FAR_FIRST:
-        send(qbuf, pp.at[core, rows32(chip), :], gath_s, gath_r.at[chip], in_plane(*step)[1])
-    pltpu.make_async_copy(qbuf, pp.at[core, rows32(chip), :], gath_r.at[chip]).start()
-    for step in ((0, 0), *FAR_FIRST):
-        c = in_plane(*step)[0]
-        part = pp.at[core, rows32(c), :]
-        wait_bytes(part, gath_r.at[c])
-        send(part, part, back_s, back_r, other)
-    wait_bytes(pb, back_r)
-
-    def build(n, _):
-        re, im = pp[0, rows32(n), :].reshape(2, 16, 512), pp[1, rows32(n), :].reshape(2, 16, 512)
-        m2[0, n, :, :, 0:512] = re
-        m2[0, n, :, :, 512:1024] = -im
-        m2[1, n, :, :, 0:512] = im
-        m2[1, n, :, :, 512:1024] = re
-        return 0
-
-    lax.fori_loop(0, 16, build, 0)
-    wait_bytes(x1, load_sem)
+    for t in range(2):
+        send(p_ref.at[1 - core, :, t], pb.at[t], pair_s, pair_r.at[t], other)
+
+    for t in range(2):
+        wait_bytes(mine.at[t], local_sem.at[t])
+        wait_bytes(pb.at[t], pair_r.at[t])
+
+        def pick(n, _, t=t):
+            half[t, n] = jnp.where(from_me, mine[t, n], pb[t, n])
+            return 0
+
+        lax.fori_loop(0, 16, pick, 0)
+        for step in FAR_FIRST:
+            c, to = in_plane(*step)
+            send(half.at[t, c], rb[t].at[chip], plane_s.at[t], plane_r.at[t], to)
+        pltpu.make_async_copy(half.at[t, chip], rb[t].at[chip], plane_r.at[t]).start()
+
+    for t in range(2):
+        wait_bytes(rb[t], plane_r.at[t])
+        cbuf[t] = rb[t][owner_chip]
+
+        def scatter_z(d, _, t=t):
+            to = (x_lo * 16 + zgroup * 4 + (member + d) % 4, col)
+            send(cbuf.at[t, :, lanes128((member + d) % 4)], zb[t].at[member], zgrp_s.at[t], zgrp_r.at[t], to)
+            return 0
+
+        lax.fori_loop(1, 4, scatter_z, 0)
+        pltpu.make_async_copy(cbuf.at[t, :, lanes128(member)], zb[t].at[member], zgrp_r.at[t]).start()
+    for t in range(2):
+        wait_bytes(zb[t], zgrp_r.at[t])
+        dbuf[t] = zb[t][lax.rem(owner_z, 4)]
+
+        def gather_z(d, _, t=t):
+            dz = 8 + jnp.where(d % 2 == 0, d // 2, -((d + 1) // 2))
+            send(dbuf.at[t], zg[t].at[z], zall_s.at[t], zall_r.at[t], (x_lo * 16 + (z + dz) % 16, col))
+            return 0
+
+        lax.fori_loop(0, 15, gather_z, 0)
+        pltpu.make_async_copy(dbuf.at[t], zg[t].at[z], zall_r.at[t]).start()
+
+    for t in range(2):
+        wait_bytes(zg[t], zall_r.at[t])
+        for m in range(4):
+            qbuf[t, :, m * 128 : (m + 1) * 128] = zg[t][lax.div(owner_z, 4) * 4 + m]
+        for step in FAR_FIRST:
+            send(qbuf.at[t], pp.at[core, t, chip], gath_s.at[t], gath_r.at[t, chip], in_plane(*step)[1])
+        pltpu.make_async_copy(qbuf.at[t], pp.at[core, t, chip], gath_r.at[t, chip]).start()
+
+    def gather_pair(t):
+        for step in ((0, 0), *FAR_FIRST):
+            c = in_plane(*step)[0]
+            part = pp.at[core, t, c]
+            wait_bytes(part, gath_r.at[t, c])
+            send(part, part, back_s, back_r.at[t], other)
+        wait_bytes(pb.at[t], back_r.at[t])
+
+        def build(n, _):
+            re, im = pp[0, t, n], pp[1, t, n]
+            m2[0, n, t, :, 0:512] = re
+            m2[0, n, t, :, 512:1024] = -im
+            m2[1, n, t, :, 0:512] = im
+            m2[1, n, t, :, 512:1024] = re
+            return 0
+
+        lax.fori_loop(0, 16, build, 0)
 
     def contract_k(q):
         h, ch = q // 2, q % 2
@@ -195,7 +200,7 @@
 
         lax.fori_loop(0, 4, swap_in, 0)
 
-        for dx, dz in ((1, 1), (0, 1), (1, 0), (0, 0)):
+        for dx, dz in ((0, 1), (1, 1), (1, 0), (0, 0)):
             to_x, to_half = (x_lo + dx) % 2, (zhalf + dz) % 2
             hi = to_x * 2 + to_half
             y = lax.dot_general(
@@ -214,11 +219,15 @@
             lax.fori_loop(0 if dx or dz else 1, 8, scatter_row, 0)
         pltpu.make_async_copy(sb.at[q, row], r2.at[q, row], row_r.at[q]).start()
 
+    gather_pair(0)
+    wait_bytes(x1, load_sem)
     contract_k(0)
     exchange_col(0)
-    for q in (1, 2, 3):
-        contract_k(q)
+    gather_pair(1)
+    contract_k(1)
     exchange_col(1)
+    contract_k(2)
+    contract_k(3)
     contract_j(0)
     exchange_col(2)
     contract_j(1)
@@ -272,11 +281,12 @@
         lax.fori_loop(0, 4, contract_i, 0)
 
     wait_bytes(pb, pair_s)
-    wait_bytes(rb.at[pl.ds(0, 15)], plane_s)
-    wait_bytes(zb.at[pl.ds(0, 3)], zgrp_s)
-    wait_bytes(zg.at[pl.ds(0, 15)], zall_s)
-    wait_bytes(rb.at[pl.ds(0, 15)], gath_s)
     wait_bytes(pb, back_s)
+    for t in range(2):
+        wait_bytes(rb[t].at[pl.ds(0, 15)], plane_s.at[t])
+        wait_bytes(zb[t].at[pl.ds(0, 3)], zgrp_s.at[t])
+        wait_bytes(zg[t].at[pl.ds(0, 15)], zall_s.at[t])
+        wait_bytes(rb[t].at[pl.ds(0, 15)], gath_s.at[t])
     for q in range(4):
         wait_bytes(r1.at[q, pl.ds(0, 15)], col_s.at[q])
         wait_bytes(r2.at[q, pl.ds(0, 31)], row_s.at[q])
@@ -312,16 +322,19 @@
         ],
         out_specs=(held, held, held),
         scratch_shapes=[
-            vmem((512, 512), BF16),
-            vmem((512, 512), BF16),
-            vmem((512, 512), BF16),
-            vmem((16, 32, 512), BF16),
-            vmem((32, 512), BF16),
-            vmem((4, 32, 128), BF16),
-            vmem((32, 128), BF16),
-            vmem((16, 32, 128), BF16),
-            vmem((32, 512), BF16),
-            vmem((2, 512, 512), BF16),
+            vmem((2, 16, 16, 512), BF16),
+            vmem((2, 16, 16, 512), BF16),
+            vmem((2, 16, 16, 512), BF16),
+            vmem((16, 16, 512), BF16),
+            vmem((16, 16, 512), BF16),
+            vmem((2, 16, 512), BF16),
+            vmem((4, 16, 128), BF16),
+            vmem((4, 16, 128), BF16),
+            vmem((2, 16, 128), BF16),
+            vmem((16, 16, 128), BF16),
+            vmem((16, 16, 128), BF16),
+            vmem((2, 16, 512), BF16),
+            vmem((2, 2, 16, 16, 512), BF16),
             vmem((2, 16, 2, 16, 1024), BF16),
             vmem((1024, 512), BF16),
             vmem((512, 1024), BF16),
@@ -330,11 +343,12 @@
             vmem((128, 1024), BF16),
             vmem((4, 32, 2, 16, 128), BF16),
             vmem((4, 32, 2, 16, 128), BF16),
-            dma, dma, dma, dma, dma, dma, dma, dma, dma, dma((16,)), dma, dma,
-            dma, dma, dma((4,)), dma((4, 4)), dma((4,)), dma((4,)),
+            dma, dma((2,)), dma((2,)), dma((2,)), dma((2,)), dma((2,)), dma((2,)), dma((2,)), dma((2,)), dma((2, 16)),
+            dma, dma((2,)),
+            dma((2,)), dma, dma((4,)), dma((4, 4)), dma((4,)), dma((4,)),
         ],
         compiler_params=pltpu.CompilerParams(collective_id=0, has_side_effects=True, vmem_limit_bytes=60 << 20),
-    )(source_owner, elemental.reshape(2, 512, 512), perambulators[0])
+    )(source_owner, elemental.reshape(2, 512, 512), perambulators.reshape(2, 16, 2, 16, 512))
     out = pl.pallas_call(
         finish,
         out_shape=jax.ShapeDtypeStruct((2, 16, 32, 512), F32),

time: 108 us -> 102 us (0.944)
  Pallas kernels: 106 us -> 99.8 us
    pallas_call x1, Pallas kernels: 104 us -> 98.2 us  [per_device(): pl.pallas_call(kernel, out_shape=(vmem((2, 2, 16, 16, 512), F32), vmem((2...]
where the time goes in v3:
time: 102 us; the launch traced here: 100 us
  Pallas kernels  99.8 us (98%)
    pallas_call x1, Pallas kernels, per_device(): pl.pallas_call(kernel, out_shape=(vmem((2, 2, 16, 16, 512), F32), vmem((2...  98.2 us

profile of v3, /device:TPU:1, one launch (start us, length us, event | category | flops | bytes accessed | tf_op | source)
XLA Modules:
  0.0 100.5 jit_solution(817424212134806898)
XLA Ops:
  0.7 98.2 %shard_map.37 = (f32[2,2,16,16,512]{4,3,2,1,0:T(8,128)S(1)}, bf16[256,512]{1,0:T(8,128)(2,1)S(1)}, bf16[1024,512]{1,0:T(8,128)(2,1)S(1)}) custom-call(s32[1]{0:T(128)S(6)} %copy.4.own_ref, bf16[2,512,512]{2,1,0:T(8,128)(2,1)} %bitcast.3, bf16[2,16,2,16,512]{4,3,2,1,0:T(8,128)(2,1)} %bitcast.4), custom_call_target="tpu_custom_call" | custom-call | tf_op jit(solution)/shard_map/pallas_call | solution.py:315
  98.8 1.6 %shard_map.38 = f32[2,16,32,512]{3,2,1,0:T(8,128)} custom-call(f32[2,2,16,16,512]{4,3,2,1,0:T(8,128)S(1)} %get-tuple-element.8.acc, bf16[256,512]{1,0:T(8,128)(2,1)S(1)} %get-tuple-element.9.x3, bf16[1024,512]{1,0:T(8,128)(2,1)S(1)} %get-tuple-element.10.m3), custom_call_target="tpu_custom_call" | custom-call | tf_op jit(solution)/shard_map/pallas_call | solution.py:352

commit v4 on v3

--- a/solution.py
+++ b/solution.py
@@ -15,6 +15,8 @@
     ((dx, dy) for dx in range(4) for dy in range(4) if dx or dy),
     key=lambda d: -(min(d[0], 4 - d[0]) + min(d[1], 4 - d[1])),
 )
+ORDER = ((0, (4, 3, 5, 6)), (1, (4, 3, 5, 6)), (1, (2, 7, 1, 0)), (0, (2, 7, 1, 0)))
+COL_FAR_FIRST = [(dh, dy, dc) for dh in (1, 0) for dy in (2, 1, 3, 0) for dc in (1, 0) if dh or dy or dc]
 
 
 def butterfly(arrs, group):
@@ -67,14 +69,15 @@
         return 0
 
     def greet_row(d, _):
-        for x in range(2):
-            greet((x * 16 + (z + d) % 16, col))
+        dz = 8 + jnp.where(d % 2 == 0, d // 2, -((d + 1) // 2))
+        for px in range(2):
+            greet((px * 16 + (z + dz) % 16, col))
         return 0
 
-    lax.fori_loop(1, 16, greet_row, 0)
     for step in FAR_FIRST:
         greet(in_plane(*step)[1])
     lax.fori_loop(0, 8, greet_other, 0)
+    lax.fori_loop(0, 15, greet_row, 0)
 
     for t in range(2):
         pltpu.make_async_copy(p_ref.at[core, :, t], mine.at[t], local_sem.at[t]).start()
@@ -175,15 +178,10 @@
             y1[q, s] = y.astype(BF16)
 
     def exchange_col(q):
-        def scatter_col(n, _):
-            k = n % 8
-            dy = jnp.where(k // 2 == 0, 2, jnp.where(k // 2 == 1, 1, jnp.where(k // 2 == 2, 3, 0)))
-            c = (((x_hi + 1 - n // 8) % 2) * 4 + (y + dy) % 4) * 2 + (core + 1 - k % 2) % 2
+        for dh, dy, dc in COL_FAR_FIRST:
+            c = (((x_hi + dh) % 2) * 4 + (y + dy) % 4) * 2 + (core + dc) % 2
             rows = pl.ds(pl.multiple_of(c * 16, 16), 16)
             send(y1.at[q, :, rows, :], r1.at[q, col], col_s.at[q], col_r.at[q, col // 4], (row, c))
-            return 0
-
-        lax.fori_loop(0, 15, scatter_col, 0)
         rows = pl.ds(pl.multiple_of(col * 16, 16), 16)
         pltpu.make_async_copy(y1.at[q, :, rows, :], r1.at[q, col], col_r.at[q, col // 4]).start()
 
@@ -200,24 +198,25 @@
 
         lax.fori_loop(0, 4, swap_in, 0)
 
-        for dx, dz in ((0, 1), (1, 1), (1, 0), (0, 0)):
-            to_x, to_half = (x_lo + dx) % 2, (zhalf + dz) % 2
-            hi = to_x * 2 + to_half
-            y = lax.dot_general(
-                x2[...], m2[:, pl.ds(hi * 4, 4)].reshape(256, 1024), NT, preferred_element_type=F32
-            ).astype(BF16)
+        for dx, steps in ORDER:
+            to_x = (x_lo + dx) % 2
+            pairs = [(z // 2 + step) % 8 for step in steps]
+            rhs = jnp.concatenate([m2[:, to_x * 8 + p].reshape(2, 32, 1024) for p in pairs], axis=1)
+            v = lax.dot_general(x2[...], rhs.reshape(256, 1024), NT, preferred_element_type=F32).astype(BF16)
             for s in range(2):
-                got = [y[k * 16 : (k + 1) * 16, s * 128 : (s + 1) * 128] for k in range(8)]
-                for k, v in enumerate(butterfly(got, 16)):
-                    sb[q, hi * 8 + k, s, :, :] = v
-
-            def scatter_row(d, _):
-                to = to_x * 16 + to_half * 8 + (zrest + d) % 8
-                send(sb.at[q, to], r2.at[q, row], row_s.at[q], row_r.at[q], (to, col))
+                got = [v[k * 16 : (k + 1) * 16, s * 128 : (s + 1) * 128] for k in range(8)]
+                for k, w in enumerate(butterfly(got, 16)):
+                    sb[q, to_x * 16 + pairs[k // 2] * 2 + k % 2, s, :, :] = w
+
+            def scatter_row(n, _):
+                k = n // 2
+                step = jnp.where(k == 0, steps[0], jnp.where(k == 1, steps[1], jnp.where(k == 2, steps[2], steps[3])))
+                to = to_x * 16 + ((z // 2 + step) % 8) * 2 + (z + 1 + n) % 2
+                send(sb.at[q, to], r2.at[q, row], row_s.at[q], row_r.at[q, x_lo], (to, col))
                 return 0
 
-            lax.fori_loop(0 if dx or dz else 1, 8, scatter_row, 0)
-        pltpu.make_async_copy(sb.at[q, row], r2.at[q, row], row_r.at[q]).start()
+            lax.fori_loop(0, 8 if dx or steps[3] else 7, scatter_row, 0)
+        pltpu.make_async_copy(sb.at[q, row], r2.at[q, row], row_r.at[q, x_lo]).start()
 
     gather_pair(0)
     wait_bytes(x1, load_sem)
@@ -254,16 +253,17 @@
 
     for q in range(4):
         ch = q % 2
-        wait_bytes(r2.at[q], row_r.at[q])
-
-        def swap_out(n, _, q=q):
-            r, x = n // 2, n % 2
-            got = [r2[q, x * 16 + k, r, :, :] for k in range(16)]
-            for k, v in enumerate(butterfly(got, 1)):
-                x3[k * 16 : (k + 1) * 16, lanes128(n)] = v
-            return 0
-
-        lax.fori_loop(0, 4, swap_out, 0)
+        for dx in (1, 0):
+            from_x = (x_lo + dx) % 2
+            wait_bytes(r2.at[q, pl.ds(from_x * 16, 16)], row_r.at[q, from_x])
+
+            def swap_out(r, _, q=q, from_x=from_x):
+                got = [r2[q, from_x * 16 + k, r, :, :] for k in range(16)]
+                for k, v in enumerate(butterfly(got, 1)):
+                    x3[k * 16 : (k + 1) * 16, lanes128(r * 2 + from_x)] = v
+                return 0
+
+            lax.fori_loop(0, 2, swap_out, 0)
         if q == 3:
             break
         m3 = (m3a, m3b)[q // 2]
@@ -345,7 +345,7 @@
             vmem((4, 32, 2, 16, 128), BF16),
             dma, dma((2,)), dma((2,)), dma((2,)), dma((2,)), dma((2,)), dma((2,)), dma((2,)), dma((2,)), dma((2, 16)),
             dma, dma((2,)),
-            dma((2,)), dma, dma((4,)), dma((4, 4)), dma((4,)), dma((4,)),
+            dma((2,)), dma, dma((4,)), dma((4, 4)), dma((4,)), dma((4, 2)),
         ],
         compiler_params=pltpu.CompilerParams(collective_id=0, has_side_effects=True, vmem_limit_bytes=60 << 20),
     )(source_owner, elemental.reshape(2, 512, 512), perambulators.reshape(2, 16, 2, 16, 512))

time: 102 us -> 103 us (level)
  Pallas kernels: 99.8 us -> 102 us
    pallas_call x1, Pallas kernels: 98.2 us -> 100 us  [per_device(): pl.pallas_call(kernel, out_shape=(vmem((2, 2, 16, 16, 512), F32), vmem((2...]
where the time goes in v4:
time: 103 us; the launch traced here: 102 us
  Pallas kernels  102 us (99%)
    pallas_call x1, Pallas kernels, per_device(): pl.pallas_call(kernel, out_shape=(vmem((2, 2, 16, 16, 512), F32), vmem((2...  100 us

profile of v4, /device:TPU:1, one launch (start us, length us, event | category | flops | bytes accessed | tf_op | source)
XLA Modules:
  0.0 102.4 jit_solution(15305368301651469104)
XLA Ops:
  0.7 100.2 %shard_map.37 = (f32[2,2,16,16,512]{4,3,2,1,0:T(8,128)S(1)}, bf16[256,512]{1,0:T(8,128)(2,1)S(1)}, bf16[1024,512]{1,0:T(8,128)(2,1)S(1)}) custom-call(s32[1]{0:T(128)S(6)} %copy.4.own_ref, bf16[2,512,512]{2,1,0:T(8,128)(2,1)} %bitcast.3, bf16[2,16,2,16,512]{4,3,2,1,0:T(8,128)(2,1)} %bitcast.4), custom_call_target="tpu_custom_call" | custom-call | tf_op jit(solution)/shard_map/pallas_call | solution.py:315
  100.8 1.6 %shard_map.38 = f32[2,16,32,512]{3,2,1,0:T(8,128)} custom-call(f32[2,2,16,16,512]{4,3,2,1,0:T(8,128)S(1)} %get-tuple-element.8.acc, bf16[256,512]{1,0:T(8,128)(2,1)S(1)} %get-tuple-element.9.x3, bf16[1024,512]{1,0:T(8,128)(2,1)S(1)} %get-tuple-element.10.m3), custom_call_target="tpu_custom_call" | custom-call | tf_op jit(solution)/shard_map/pallas_call | solution.py:352

commit v5 on v4

--- a/solution.py
+++ b/solution.py
@@ -74,10 +74,10 @@
             greet((px * 16 + (z + dz) % 16, col))
         return 0
 
+    lax.fori_loop(0, 15, greet_row, 0)
     for step in FAR_FIRST:
         greet(in_plane(*step)[1])
     lax.fori_loop(0, 8, greet_other, 0)
-    lax.fori_loop(0, 15, greet_row, 0)
 
     for t in range(2):
         pltpu.make_async_copy(p_ref.at[core, :, t], mine.at[t], local_sem.at[t]).start()

time: 103 us -> 101 us (0.981)
  Pallas kernels: 102 us -> 100 us
    pallas_call x1, Pallas kernels: 100 us -> 98.4 us  [per_device(): pl.pallas_call(kernel, out_shape=(vmem((2, 2, 16, 16, 512), F32), vmem((2...]
where the time goes in v5:
time: 101 us
  Pallas kernels  100 us (99%)
    pallas_call x1, Pallas kernels, per_device(): pl.pallas_call(kernel, out_shape=(vmem((2, 2, 16, 16, 512), F32), vmem((2...  98.4 us

profile of v5, /device:TPU:1, one launch (start us, length us, event | category | flops | bytes accessed | tf_op | source)
XLA Modules:
  0.0 100.7 jit_solution(2621489699520297888)
XLA Ops:
  0.7 98.4 %shard_map.37 = (f32[2,2,16,16,512]{4,3,2,1,0:T(8,128)S(1)}, bf16[256,512]{1,0:T(8,128)(2,1)S(1)}, bf16[1024,512]{1,0:T(8,128)(2,1)S(1)}) custom-call(s32[1]{0:T(128)S(6)} %copy.4.own_ref, bf16[2,512,512]{2,1,0:T(8,128)(2,1)} %bitcast.3, bf16[2,16,2,16,512]{4,3,2,1,0:T(8,128)(2,1)} %bitcast.4), custom_call_target="tpu_custom_call" | custom-call | tf_op jit(solution)/shard_map/pallas_call | solution.py:315
  99.1 1.6 %shard_map.38 = f32[2,16,32,512]{3,2,1,0:T(8,128)} custom-call(f32[2,2,16,16,512]{4,3,2,1,0:T(8,128)S(1)} %get-tuple-element.8.acc, bf16[256,512]{1,0:T(8,128)(2,1)S(1)} %get-tuple-element.9.x3, bf16[1024,512]{1,0:T(8,128)(2,1)S(1)} %get-tuple-element.10.m3), custom_call_target="tpu_custom_call" | custom-call | tf_op jit(solution)/shard_map/pallas_call | solution.py:352
